TPU v7x, 32 devices: a whole 2x2x4 slice. The times are simulated.
32 devices in a mesh: gx: 4 (over z), gy: 8 (over y, x, core).
Axes of the slice: x: 2, y: 2, z: 4, core: 2. Of those that a mesh axis runs over, the one named last changes fastest.
Arguments:
- features: bfloat16 [8192, 512], P(('gx', 'gy')), may hold values from -6 to 6
- cotangent: bfloat16 [8192, 512], P(('gx', 'gy')), may hold values from -6 to 6
- self_weight: bfloat16 [3, 512, 512], replicated, may hold values from -0.25 to 0.25
- neigh_weight: bfloat16 [3, 512, 512], replicated, may hold values from -0.25 to 0.25
- block_val: bfloat16 [64, 4, 128, 128], P(('gx', 'gy')), may hold values from -0.25 to 0.25
- block_col: int32 [64, 4], P(('gx', 'gy')), may hold values from 0 to 5
- send_idx: int32 [32, 32, 16], P(('gx', 'gy')), may hold values from 0 to 255
- send_count: int32 [32, 32], P(('gx', 'gy')), may hold values from 0 to 16, as said below
Outputs:
- self_grad: bfloat16 [3, 512, 512], replicated
- neigh_grad: bfloat16 [3, 512, 512], replicated
- input_grad: bfloat16 [8192, 512], P(('gx', 'gy'))
Inputs may be any that keep to these rules, and one draw needn't show every extreme that they name: `send_count`: at most 16 rows from one device to one peer; in every draw some receivers get exactly 16 from every device.
All inputs are finite; a program needn't handle non-finite values.
Results may differ from a plain program's by a relative error of at most 0.02.
Values may be sent and summed in bfloat16 or wider, within the bound.
No kernel may reach another device: no remote copies, remote signals or barrier semaphores. Data moves between devices by JAX's collectives and lax.ppermute only.
A program may use at most 128 MiB of HBM per device.

v0:
```python
import math
import jax
import jax.numpy as jnp
from jax import lax
from jax.sharding import PartitionSpec as P


def gather_sum(extended, values, columns, tile):
    width = extended.shape[1]
    tiled = extended.reshape(-1, tile, width)[columns]
    total = jnp.einsum("rbij,rbjd->rid", values, tiled, preferred_element_type=jnp.float32)
    return total.reshape(-1, width)


def spread_back(upstream, values, columns, ext_tiles, tile):
    width = upstream.shape[1]
    contrib = jnp.einsum(
        "rbij,rid->rbjd",
        values,
        upstream.reshape(-1, tile, width),
        preferred_element_type=jnp.float32,
    )
    onehot = (
        columns.reshape(-1)[None, :] == jnp.arange(ext_tiles, dtype=jnp.int32)[:, None]
    ).astype(jnp.float32)
    total = jnp.einsum(
        "cn,njd->cjd", onehot, contrib.reshape(-1, tile, width), precision=lax.Precision.HIGHEST
    )
    return total.reshape(-1, width)


def per_device(
    features, cotangent, self_weight, neigh_weight, block_val, block_col, send_idx, send_count
):
    outer = lax.axis_size("gx")
    inner = lax.axis_size("gy")
    devices = outer * inner
    node_rows, width = features.shape
    tile = block_val.shape[2]
    layers = self_weight.shape[0]
    slots = send_idx.shape[2]
    halo_rows = devices * slots
    ext_tiles = (node_rows + halo_rows) // tile
    scale = 1.0 / math.sqrt(node_rows * devices)
    row_ids = send_idx.reshape(-1)
    live = (jnp.arange(slots, dtype=jnp.int32)[None, :] < send_count.reshape(-1)[:, None]).reshape(
        -1, 1
    )
    hiddens = [features]
    aggregates = []
    preacts = []
    hidden = features
    for layer_at in range(layers):
        picked = jnp.where(live, jnp.take(hidden, row_ids, axis=0), jnp.zeros((), hidden.dtype))
        picked = picked.reshape(outer, inner, slots, width)
        send_arrived = lax.all_to_all(
            lax.all_to_all(picked, "gx", split_axis=0, concat_axis=0, tiled=True),
            "gy",
            split_axis=1,
            concat_axis=1,
            tiled=True,
        )
        extended = jnp.concatenate([hidden, send_arrived.reshape(halo_rows, width)], axis=0)
        aggregate = gather_sum(extended, block_val, block_col, tile).astype(jnp.bfloat16)
        preact = jnp.dot(
            hidden, self_weight[layer_at], preferred_element_type=jnp.float32
        ) + jnp.dot(aggregate, neigh_weight[layer_at], preferred_element_type=jnp.float32)
        aggregates.append(aggregate)
        preacts.append(preact)
        if layer_at < layers - 1:
            hidden = jax.nn.silu(preact).astype(jnp.bfloat16)
            hiddens.append(hidden)
    transposed = (((0,), (0,)), ((), ()))
    against = (((1,), (1,)), ((), ()))
    self_list = [None] * layers
    neigh_list = [None] * layers
    grad = cotangent
    for layer_at in reversed(range(layers)):
        preact = preacts[layer_at]
        sigma = jax.nn.sigmoid(preact)
        delta = (grad.astype(jnp.float32) * sigma * (1.0 + preact * (1.0 - sigma))).astype(
            jnp.bfloat16
        )
        self_term = lax.dot_general(
            hiddens[layer_at], delta, transposed, preferred_element_type=jnp.float32
        )
        neigh_term = lax.dot_general(
            aggregates[layer_at], delta, transposed, preferred_element_type=jnp.float32
        )
        self_sum, neigh_sum = lax.psum((self_term, neigh_term), ("gx", "gy"))
        self_list[layer_at] = (self_sum * scale).astype(jnp.bfloat16)
        neigh_list[layer_at] = (neigh_sum * scale).astype(jnp.bfloat16)
        own_part = lax.dot_general(
            delta, self_weight[layer_at], against, preferred_element_type=jnp.float32
        )
        upstream = lax.dot_general(
            delta, neigh_weight[layer_at], against, preferred_element_type=jnp.float32
        ).astype(jnp.bfloat16)
        ext_grad = spread_back(upstream, block_val, block_col, ext_tiles, tile)
        outgoing = ext_grad[node_rows:].astype(jnp.bfloat16).reshape(outer, inner, slots, width)
        arrived = lax.all_to_all(
            lax.all_to_all(outgoing, "gx", split_axis=0, concat_axis=0, tiled=True),
            "gy",
            split_axis=1,
            concat_axis=1,
            tiled=True,
        )
        masked = jnp.where(
            live, arrived.reshape(halo_rows, width).astype(jnp.float32), jnp.zeros((), jnp.float32)
        )
        returned = jnp.zeros((node_rows, width), jnp.float32).at[row_ids].add(masked)
        grad = (own_part + ext_grad[:node_rows] + returned).astype(jnp.bfloat16)
    self_grad = jnp.stack(self_list)
    neigh_grad = jnp.stack(neigh_list)
    return (self_grad, neigh_grad, grad)


def solution(mesh):
    return jax.shard_map(
        per_device,
        mesh=mesh,
        in_specs=(
            P(("gx", "gy"), None),
            P(("gx", "gy"), None),
            P(),
            P(),
            P(("gx", "gy"), None, None, None),
            P(("gx", "gy"), None),
            P(("gx", "gy"), None, None),
            P(("gx", "gy"), None),
        ),
        out_specs=(P(), P(), P(("gx", "gy"), None)),
        check_vma=False,
    )
```

profile of v0, /device:TPU:0, one launch (start us, length us, event | category | flops | bytes accessed | tf_op | source)
XLA Modules:
  0.0 399.9 jit_solution(2928996028955188981)
XLA Ops:
  12.1 20.8 %all_to_all.60 = bf16[4,8,16,512]{3,2,1,0:T(8,128)(2,1)S(1)} all-to-all(bf16[4,8,16,512]{3,2,1,0:T(8,128)(2,1)S(1)} %bitcast.184), channel_id=1, replica_groups=mesh['gx'=4,'gy'=8] {'gx'}, dimensions={0} | all-to-all | bytes 1048576 | tf_op jit(solution)/shard_map/all_to_all | solution.py:57
  33.7 3.7 all-to-all-start.1
  38.7 8.5 %all-to-all-done.1 = bf16[4,8,16,512]{3,2,0,1:T(8,128)(2,1)S(1)} async-done(((bf16[4,8,16,512]{3,2,0,1:T(8,128)(2,1)}), bf16[4,8,16,512]{3,2,0,1:T(8,128)(2,1)S(1)}, u32[]{:S(2)}, u32[]{:S(2)}) %all-to-all-start.1) | async-done | bytes 524320 | tf_op jit(solution)/shard_map/all_to_all | solution.py:56
  54.9 14.9 %all_to_all.61 = bf16[4,8,16,512]{3,2,1,0:T(8,128)(2,1)S(1)} all-to-all(bf16[4,8,16,512]{3,2,1,0:T(8,128)(2,1)S(1)} %bitcast.185), channel_id=1, replica_groups=mesh['gx'=4,'gy'=8] {'gx'}, dimensions={0} | all-to-all | bytes 1048576 | tf_op jit(solution)/shard_map/all_to_all | solution.py:57
  70.7 4.3 %all-to-all-start.3 = ((bf16[4,8,16,512]{3,2,0,1:T(8,128)(2,1)}), bf16[4,8,16,512]{3,2,0,1:T(8,128)(2,1)S(1)}, u32[]{:S(2)}, u32[]{:S(2)}) async-start(bf16[4,8,16,512]{3,2,0,1:T(8,128)(2,1)} %copy.111), calls=%async_computation.3 | async-start | bytes 1048576 | tf_op jit(solution)/shard_map/all_to_all | solution.py:56
  76.1 8.6 %all-to-all-done.3 = bf16[4,8,16,512]{3,2,0,1:T(8,128)(2,1)S(1)} async-done(((bf16[4,8,16,512]{3,2,0,1:T(8,128)(2,1)}), bf16[4,8,16,512]{3,2,0,1:T(8,128)(2,1)S(1)}, u32[]{:S(2)}, u32[]{:S(2)}) %all-to-all-start.3) | async-done | bytes 524320 | tf_op jit(solution)/shard_map/all_to_all | solution.py:56
  92.4 14.9 %all_to_all.62 = bf16[4,8,16,512]{3,2,1,0:T(8,128)(2,1)S(1)} all-to-all(bf16[4,8,16,512]{3,2,1,0:T(8,128)(2,1)S(1)} %bitcast.183), channel_id=1, replica_groups=mesh['gx'=4,'gy'=8] {'gx'}, dimensions={0} | all-to-all | bytes 1048576 | tf_op jit(solution)/shard_map/all_to_all | solution.py:57
  108.2 4.3 %all-to-all-start.5 = ((bf16[4,8,16,512]{3,2,0,1:T(8,128)(2,1)}), bf16[4,8,16,512]{3,2,0,1:T(8,128)(2,1)S(1)}, u32[]{:S(2)}, u32[]{:S(2)}) async-start(bf16[4,8,16,512]{3,2,0,1:T(8,128)(2,1)} %copy.113), calls=%async_computation.5 | async-start | bytes 1048576 | tf_op jit(solution)/shard_map/all_to_all | solution.py:56
  113.7 8.5 %all-to-all-done.5 = bf16[4,8,16,512]{3,2,0,1:T(8,128)(2,1)S(1)} async-done(((bf16[4,8,16,512]{3,2,0,1:T(8,128)(2,1)}), bf16[4,8,16,512]{3,2,0,1:T(8,128)(2,1)S(1)}, u32[]{:S(2)}, u32[]{:S(2)}) %all-to-all-start.5) | async-done | bytes 524320 | tf_op jit(solution)/shard_map/all_to_all | solution.py:56
  133.5 4.1 %all-to-all-start.6 = ((bf16[4,8,16,512]{3,2,1,0:T(8,128)(2,1)}), bf16[4,8,16,512]{3,2,1,0:T(8,128)(2,1)}, u32[]{:S(2)}, u32[]{:S(2)}) async-start(bf16[4,8,16,512]{3,2,1,0:T(8,128)(2,1)} %copy.119), calls=%async_computation.6 | async-start | bytes 1048576 | tf_op jit(solution)/shard_map/all_to_all | solution.py:102
  137.7 12.5 %all-to-all-done.6 = bf16[4,8,16,512]{3,2,1,0:T(8,128)(2,1)} async-done(((bf16[4,8,16,512]{3,2,1,0:T(8,128)(2,1)}), bf16[4,8,16,512]{3,2,1,0:T(8,128)(2,1)}, u32[]{:S(2)}, u32[]{:S(2)}) %all-to-all-start.6) | async-done | bytes 524320 | tf_op jit(solution)/shard_map/all_to_all | solution.py:102
  152.1 4.3 %all-to-all-start.7 = ((bf16[4,8,16,512]{3,2,0,1:T(8,128)(2,1)}), bf16[4,8,16,512]{3,2,0,1:T(8,128)(2,1)}, u32[]{:S(2)}, u32[]{:S(2)}) async-start(bf16[4,8,16,512]{3,2,0,1:T(8,128)(2,1)} %copy.120), calls=%async_computation.7 | async-start | bytes 1048576 | tf_op jit(solution)/shard_map/all_to_all | solution.py:101
  158.1 8.1 %all-to-all-done.7 = bf16[4,8,16,512]{3,2,0,1:T(8,128)(2,1)} async-done(((bf16[4,8,16,512]{3,2,0,1:T(8,128)(2,1)}), bf16[4,8,16,512]{3,2,0,1:T(8,128)(2,1)}, u32[]{:S(2)}, u32[]{:S(2)}) %all-to-all-start.7) | async-done | bytes 524320 | tf_op jit(solution)/shard_map/all_to_all | solution.py:101
  167.5 4.0 scatter_fusion
  179.6 4.1 %all-to-all-start.8 = ((bf16[4,8,16,512]{3,2,1,0:T(8,128)(2,1)}), bf16[4,8,16,512]{3,2,1,0:T(8,128)(2,1)}, u32[]{:S(2)}, u32[]{:S(2)}) async-start(bf16[4,8,16,512]{3,2,1,0:T(8,128)(2,1)} %copy.125), calls=%async_computation.8 | async-start | bytes 1048576 | tf_op jit(solution)/shard_map/all_to_all | solution.py:102
  189.1 7.2 %all-to-all-done.8 = bf16[4,8,16,512]{3,2,1,0:T(8,128)(2,1)} async-done(((bf16[4,8,16,512]{3,2,1,0:T(8,128)(2,1)}), bf16[4,8,16,512]{3,2,1,0:T(8,128)(2,1)}, u32[]{:S(2)}, u32[]{:S(2)}) %all-to-all-start.8) | async-done | bytes 524320 | tf_op jit(solution)/shard_map/all_to_all | solution.py:102
  198.2 4.3 %all-to-all-start.9 = ((bf16[4,8,16,512]{3,2,0,1:T(8,128)(2,1)}), bf16[4,8,16,512]{3,2,0,1:T(8,128)(2,1)S(1)}, u32[]{:S(2)}, u32[]{:S(2)}) async-start(bf16[4,8,16,512]{3,2,0,1:T(8,128)(2,1)} %copy.126), calls=%async_computation.9 | async-start | bytes 1048576 | tf_op jit(solution)/shard_map/all_to_all | solution.py:101
  205.2 7.0 %all-to-all-done.9 = bf16[4,8,16,512]{3,2,0,1:T(8,128)(2,1)S(1)} async-done(((bf16[4,8,16,512]{3,2,0,1:T(8,128)(2,1)}), bf16[4,8,16,512]{3,2,0,1:T(8,128)(2,1)S(1)}, u32[]{:S(2)}, u32[]{:S(2)}) %all-to-all-start.9) | async-done | bytes 524320 | tf_op jit(solution)/shard_map/all_to_all | solution.py:101
  212.5 4.0 %scatter_fusion.1 = f32[256,512]{1,0:T(8,128)S(1)} fusion(f32[256,512]{1,0:T(8,128)S(1)} %convolution_add_fusion.1, s32[512]{0:T(512)S(1)} %bitcast.199, f32[512,512]{1,0:T(8,128)S(1)} %bitcast_select_fusion.1), kind=kCustom, calls=%fused_computation.7 | custom fusion | flops 262144 | bytes 3147776 | tf_op jit(solution)/shard_map/scatter-add | solution.py:111
  226.5 22.2 %all_to_all.63 = bf16[4,8,16,512]{3,2,1,0:T(8,128)(2,1)S(1)} all-to-all(bf16[4,8,16,512]{3,2,1,0:T(8,128)(2,1)S(1)} %copy.136), channel_id=1, replica_groups=mesh['gx'=4,'gy'=8] {'gx'}, dimensions={0} | all-to-all | bytes 1048576 | tf_op jit(solution)/shard_map/all_to_all | solution.py:102
  249.5 3.5 all-to-all-start.11
  254.8 7.9 %all-to-all-done.11 = bf16[4,8,16,512]{3,2,0,1:T(8,128)(2,1)S(1)} async-done(((bf16[4,8,16,512]{3,2,0,1:T(8,128)(2,1)}), bf16[4,8,16,512]{3,2,0,1:T(8,128)(2,1)S(1)}, u32[]{:S(2)}, u32[]{:S(2)}) %all-to-all-start.11) | async-done | bytes 524320 | tf_op jit(solution)/shard_map/all_to_all | solution.py:101
  263.0 3.8 scatter_fusion.2
  267.5 117.8 %all-reduce.3.cloned.1.call-done = (f32[512,512]{0,1:T(8,128)}, f32[512,512]{0,1:T(8,128)}, f32[512,512]{0,1:T(8,128)}, f32[512,512]{0,1:T(8,128)}, f32[512,512]{0,1:T(8,128)}, /*index=5*/f32[512,512]{0,1:T(8,128)}) async-done(((f32[512,512]{0,1:T(8,128)}, f32[512,512]{0,1:T(8,128)}, f32[512,512]{0,1:T(8,128)}, f32[512,512]{0,1:T(8,128)}, f32[512,512]{0,1:T(8,128)}, /*index=5*/f32[512,512]{0,1:T(8,128)}), ...) | async-done | bytes 6291472 | tf_op jit(solution)/shard_map/psum | solution.py:90
  (132 shorter events, 81.8 us)
Async XLA Ops:
  7.2 41.7 %copy-start = (bf16[2,4,128,128]{3,2,1,0:T(8,128)(2,1)S(1)}, bf16[2,4,128,128]{3,2,1,0:T(8,128)(2,1)}, u32[]{:S(2)}) copy-start(bf16[2,4,128,128]{3,2,1,0:T(8,128)(2,1)} %param.14) | copy-start | bytes 786436
  12.1 25.4 %copy-start.17 = (s32[2,4]{1,0:T(2,128)S(1)}, s32[2,4]{1,0:T(2,128)}, u32[]{:S(2)}) copy-start(s32[2,4]{1,0:T(2,128)} %param.15) | copy-start | bytes 100
  12.1 25.5 %copy-start.1 = (bf16[256,512]{1,0:T(8,128)(2,1)S(1)}, bf16[256,512]{1,0:T(8,128)(2,1)}, u32[]{:S(2)}) copy-start(bf16[256,512]{1,0:T(8,128)(2,1)} %param.10) | copy-start | bytes 786436
  12.1 25.4 %copy-start.2 = (bf16[3,512,512]{2,1,0:T(8,128)(2,1)S(1)}, bf16[3,512,512]{2,1,0:T(8,128)(2,1)}, u32[]{:S(2)}) copy-start(bf16[3,512,512]{2,1,0:T(8,128)(2,1)} %param.12) | copy-start | bytes 4718596
  33.7 13.4 %all-to-all-start.1 = ((bf16[4,8,16,512]{3,2,0,1:T(8,128)(2,1)}), bf16[4,8,16,512]{3,2,0,1:T(8,128)(2,1)S(1)}, u32[]{:S(2)}, u32[]{:S(2)}) async-start(bf16[4,8,16,512]{3,2,0,1:T(8,128)(2,1)} %copy.109), calls=%async_computation.1 | async-start | bytes 1048576 | tf_op jit(solution)/shard_map/all_to_all | solution.py:56
  50.5 2.3 copy-start.7
  70.7 14.0 %all-to-all-start.3 = ((bf16[4,8,16,512]{3,2,0,1:T(8,128)(2,1)}), bf16[4,8,16,512]{3,2,0,1:T(8,128)(2,1)S(1)}, u32[]{:S(2)}, u32[]{:S(2)}) async-start(bf16[4,8,16,512]{3,2,0,1:T(8,128)(2,1)} %copy.111), calls=%async_computation.3 | async-start | bytes 1048576 | tf_op jit(solution)/shard_map/all_to_all | solution.py:56
  88.0 2.3 copy-start.9
  108.2 14.0 %all-to-all-start.5 = ((bf16[4,8,16,512]{3,2,0,1:T(8,128)(2,1)}), bf16[4,8,16,512]{3,2,0,1:T(8,128)(2,1)S(1)}, u32[]{:S(2)}, u32[]{:S(2)}) async-start(bf16[4,8,16,512]{3,2,0,1:T(8,128)(2,1)} %copy.113), calls=%async_computation.5 | async-start | bytes 1048576 | tf_op jit(solution)/shard_map/all_to_all | solution.py:56
  123.3 2.3 copy-start.11
  125.6 31.2 %copy-start.3 = (bf16[256,512]{1,0:T(8,128)(2,1)}, bf16[256,512]{1,0:T(8,128)(2,1)S(1)}, u32[]{:S(2)}) copy-start(bf16[256,512]{1,0:T(8,128)(2,1)S(1)} %multiply_convert_fusion.8) | copy-start | bytes 786436
  133.5 16.7 %all-to-all-start.6 = ((bf16[4,8,16,512]{3,2,1,0:T(8,128)(2,1)}), bf16[4,8,16,512]{3,2,1,0:T(8,128)(2,1)}, u32[]{:S(2)}, u32[]{:S(2)}) async-start(bf16[4,8,16,512]{3,2,1,0:T(8,128)(2,1)} %copy.119), calls=%async_computation.6 | async-start | bytes 1048576 | tf_op jit(solution)/shard_map/all_to_all | solution.py:102
  152.1 14.1 %all-to-all-start.7 = ((bf16[4,8,16,512]{3,2,0,1:T(8,128)(2,1)}), bf16[4,8,16,512]{3,2,0,1:T(8,128)(2,1)}, u32[]{:S(2)}, u32[]{:S(2)}) async-start(bf16[4,8,16,512]{3,2,0,1:T(8,128)(2,1)} %copy.120), calls=%async_computation.7 | async-start | bytes 1048576 | tf_op jit(solution)/shard_map/all_to_all | solution.py:101
  167.5 4.0 %copy-start.13 = (f32[256,512]{1,0:T(8,128)S(1)}, f32[256,512]{1,0:T(8,128)}, u32[]{:S(2)}) copy-start(f32[256,512]{1,0:T(8,128)} %get-tuple-element.28) | copy-start | bytes 1572868
  179.6 16.7 %all-to-all-start.8 = ((bf16[4,8,16,512]{3,2,1,0:T(8,128)(2,1)}), bf16[4,8,16,512]{3,2,1,0:T(8,128)(2,1)}, u32[]{:S(2)}, u32[]{:S(2)}) async-start(bf16[4,8,16,512]{3,2,1,0:T(8,128)(2,1)} %copy.125), calls=%async_computation.8 | async-start | bytes 1048576 | tf_op jit(solution)/shard_map/all_to_all | solution.py:102
  183.7 2.4 copy-start.4
  186.1 1.7 copy-start.10
  198.2 14.0 %all-to-all-start.9 = ((bf16[4,8,16,512]{3,2,0,1:T(8,128)(2,1)}), bf16[4,8,16,512]{3,2,0,1:T(8,128)(2,1)S(1)}, u32[]{:S(2)}, u32[]{:S(2)}) async-start(bf16[4,8,16,512]{3,2,0,1:T(8,128)(2,1)} %copy.126), calls=%async_computation.9 | async-start | bytes 1048576 | tf_op jit(solution)/shard_map/all_to_all | solution.py:101
  202.5 182.8 %all-reduce.3.cloned.1.call-start = ((), (), s32[]{:S(2)}) async-start(), calls=%async_computation.12 | async-start | bytes 12582912 | tf_op jit(solution)/shard_map/psum | solution.py:90
  212.5 4.1 %copy-start.12 = (f32[256,512]{1,0:T(8,128)S(1)}, f32[256,512]{1,0:T(8,128)}, u32[]{:S(2)}) copy-start(f32[256,512]{1,0:T(8,128)} %get-tuple-element.26) | copy-start | bytes 1572868
  212.5 4.3 %copy-start.8 = (bf16[2,512,128]{1,2,0:T(8,128)(2,1)S(1)}, bf16[2,512,128]{1,2,0:T(8,128)(2,1)}, u32[]{:S(2)}) copy-start(bf16[2,512,128]{1,2,0:T(8,128)(2,1)} %copy-done.7) | copy-start | bytes 786436
  249.5 13.1 %all-to-all-start.11 = ((bf16[4,8,16,512]{3,2,0,1:T(8,128)(2,1)}), bf16[4,8,16,512]{3,2,0,1:T(8,128)(2,1)S(1)}, u32[]{:S(2)}, u32[]{:S(2)}) async-start(bf16[4,8,16,512]{3,2,0,1:T(8,128)(2,1)} %copy.137), calls=%async_computation.11 | async-start | bytes 1048576 | tf_op jit(solution)/shard_map/all_to_all | solution.py:101
  385.3 2.0 copy-start.5
  385.3 2.2 copy-start.6
  (4 other events, 5.4 us)
Sparse Core Ops, SparseCore 0:
  219.6 165.6 all-reduce.2
where the time goes:
time: 402 us; the launch traced here: 400 us
  waiting for transfers between devices  186 us (46%)
  blocking collectives  72.8 us (18%)
  matrix products  39.5 us (10%)
  local copies, waits for them, and re-layouts  34.6 us (9%)
  starting transfers between devices  32.8 us (8%)
  other arithmetic  19.4 us (5%)
  between operations  14.7 us (4%)
    psum x1, waiting for transfers between devices, per_device(): self_sum, neigh_sum = lax.psum((self_term, neigh_term), ('gx', 'gy'))  118 us
    all_to_all x3, blocking collectives, per_device(): lax.all_to_all(picked, 'gx', split_axis=0, concat_axis=0, tiled=True)  50.6 us
    all_to_all x3, waiting for transfers between devices, per_device(): lax.all_to_all(lax.all_to_all(picked, 'gx', split_axis=0, concat_axis=0,...  25.7 us
    all_to_all x3, waiting for transfers between devices, per_device(): lax.all_to_all(lax.all_to_all(outgoing, 'gx', split_axis=0, concat_axis=0...  23 us
    all_to_all x1, blocking collectives, per_device(): lax.all_to_all(outgoing, 'gx', split_axis=0, concat_axis=0, tiled=True)  22.2 us
    all_to_all x2, waiting for transfers between devices, per_device(): lax.all_to_all(outgoing, 'gx', split_axis=0, concat_axis=0, tiled=True)  19.7 us
    all_to_all x3, starting transfers between devices, per_device(): lax.all_to_all(lax.all_to_all(picked, 'gx', split_axis=0, concat_axis=0,...  12.4 us
    all_to_all x3, starting transfers between devices, per_device(): lax.all_to_all(lax.all_to_all(outgoing, 'gx', split_axis=0, concat_axis=0...  12.1 us
  transfers between devices with their start and end apart: 9, of which 9 were waited for; matrix products, arithmetic and copies ran while one was open for 7% of the time, Pallas kernels for 0%

commit v1 on v0

--- a/solution.py
+++ b/solution.py
@@ -87,7 +87,7 @@
         neigh_term = lax.dot_general(
             aggregates[layer_at], delta, transposed, preferred_element_type=jnp.float32
         )
-        self_sum, neigh_sum = lax.psum((self_term, neigh_term), ("gx", "gy"))
+        self_sum, neigh_sum = lax.psum(lax.psum((self_term, neigh_term), "gy"), "gx")
         self_list[layer_at] = (self_sum * scale).astype(jnp.bfloat16)
         neigh_list[layer_at] = (neigh_sum * scale).astype(jnp.bfloat16)
         own_part = lax.dot_general(

time: 402 us -> 574 us (1.43)
  waiting for transfers between devices: 186 us -> 346 us
  blocking collectives: 72.8 us -> 85.4 us
    psum x1 -> x2, waiting for transfers between devices: 118 us -> 277 us  [the longest x1 176 us: per_device(): lax.psum(lax.psum((self_term, neigh_term), 'gy'), 'gx')]
    all_to_all x1, blocking collectives: 22.2 us -> 34.8 us  [per_device(): lax.all_to_all(outgoing, 'gx', split_axis=0, concat_axis=0, tiled=True)]
  transfers between devices with their start and end apart: 9 -> 10, of which waited for: 9 -> 10; matrix products, arithmetic and copies ran while one was open for 7% -> 5% of each run, Pallas kernels for 0% -> 0%
where the time goes in v1:
time: 574 us; the launch traced here: 572 us
  waiting for transfers between devices  346 us (60%)
  blocking collectives  85.4 us (15%)
  matrix products  39.5 us (7%)
  local copies, waits for them, and re-layouts  34.6 us (6%)
  starting transfers between devices  33.2 us (6%)
  other arithmetic  18.8 us (3%)
  between operations  14.7 us (3%)
    psum x1, waiting for transfers between devices, per_device(): lax.psum(lax.psum((self_term, neigh_term), 'gy'), 'gx')  176 us
    psum x1, waiting for transfers between devices, per_device(): lax.psum((self_term, neigh_term), 'gy')  101 us
    all_to_all x3, blocking collectives, per_device(): lax.all_to_all(picked, 'gx', split_axis=0, concat_axis=0, tiled=True)  50.6 us
    all_to_all x1, blocking collectives, per_device(): lax.all_to_all(outgoing, 'gx', split_axis=0, concat_axis=0, tiled=True)  34.8 us
    all_to_all x3, waiting for transfers between devices, per_device(): lax.all_to_all(lax.all_to_all(picked, 'gx', split_axis=0, concat_axis=0,...  25.7 us
    all_to_all x3, waiting for transfers between devices, per_device(): lax.all_to_all(lax.all_to_all(outgoing, 'gx', split_axis=0, concat_axis=0...  23 us
    all_to_all x2, waiting for transfers between devices, per_device(): lax.all_to_all(outgoing, 'gx', split_axis=0, concat_axis=0, tiled=True)  19.7 us
    all_to_all x3, starting transfers between devices, per_device(): lax.all_to_all(lax.all_to_all(picked, 'gx', split_axis=0, concat_axis=0,...  12.4 us
  transfers between devices with their start and end apart: 10, of which 10 were waited for; matrix products, arithmetic and copies ran while one was open for 5% of the time, Pallas kernels for 0%

profile of v1, /device:TPU:0, one launch (start us, length us, event | category | flops | bytes accessed | tf_op | source)
XLA Modules:
  0.0 572.1 jit_solution(8444008624706183343)
XLA Ops:
  12.1 20.8 %all_to_all.60 = bf16[4,8,16,512]{3,2,1,0:T(8,128)(2,1)S(1)} all-to-all(bf16[4,8,16,512]{3,2,1,0:T(8,128)(2,1)S(1)} %bitcast.184), channel_id=1, replica_groups=mesh['gx'=4,'gy'=8] {'gx'}, dimensions={0} | all-to-all | bytes 1048576 | tf_op jit(solution)/shard_map/all_to_all | solution.py:57
  33.8 3.7 all-to-all-start.1
  38.7 8.5 %all-to-all-done.1 = bf16[4,8,16,512]{3,2,0,1:T(8,128)(2,1)S(1)} async-done(((bf16[4,8,16,512]{3,2,0,1:T(8,128)(2,1)}), bf16[4,8,16,512]{3,2,0,1:T(8,128)(2,1)S(1)}, u32[]{:S(2)}, u32[]{:S(2)}) %all-to-all-start.1) | async-done | bytes 524320 | tf_op jit(solution)/shard_map/all_to_all | solution.py:56
  54.9 14.9 %all_to_all.61 = bf16[4,8,16,512]{3,2,1,0:T(8,128)(2,1)S(1)} all-to-all(bf16[4,8,16,512]{3,2,1,0:T(8,128)(2,1)S(1)} %bitcast.185), channel_id=1, replica_groups=mesh['gx'=4,'gy'=8] {'gx'}, dimensions={0} | all-to-all | bytes 1048576 | tf_op jit(solution)/shard_map/all_to_all | solution.py:57
  70.7 4.3 all-to-all-start.3
  76.1 8.6 %all-to-all-done.3 = bf16[4,8,16,512]{3,2,0,1:T(8,128)(2,1)S(1)} async-done(((bf16[4,8,16,512]{3,2,0,1:T(8,128)(2,1)}), bf16[4,8,16,512]{3,2,0,1:T(8,128)(2,1)S(1)}, u32[]{:S(2)}, u32[]{:S(2)}) %all-to-all-start.3) | async-done | bytes 524320 | tf_op jit(solution)/shard_map/all_to_all | solution.py:56
  92.4 14.9 %all_to_all.62 = bf16[4,8,16,512]{3,2,1,0:T(8,128)(2,1)S(1)} all-to-all(bf16[4,8,16,512]{3,2,1,0:T(8,128)(2,1)S(1)} %bitcast.183), channel_id=1, replica_groups=mesh['gx'=4,'gy'=8] {'gx'}, dimensions={0} | all-to-all | bytes 1048576 | tf_op jit(solution)/shard_map/all_to_all | solution.py:57
  108.2 4.3 all-to-all-start.5
  113.7 8.5 %all-to-all-done.5 = bf16[4,8,16,512]{3,2,0,1:T(8,128)(2,1)S(1)} async-done(((bf16[4,8,16,512]{3,2,0,1:T(8,128)(2,1)}), bf16[4,8,16,512]{3,2,0,1:T(8,128)(2,1)S(1)}, u32[]{:S(2)}, u32[]{:S(2)}) %all-to-all-start.5) | async-done | bytes 524320 | tf_op jit(solution)/shard_map/all_to_all | solution.py:56
  133.5 4.1 all-to-all-start.6
  137.7 12.5 %all-to-all-done.6 = bf16[4,8,16,512]{3,2,1,0:T(8,128)(2,1)} async-done(((bf16[4,8,16,512]{3,2,1,0:T(8,128)(2,1)}), bf16[4,8,16,512]{3,2,1,0:T(8,128)(2,1)}, u32[]{:S(2)}, u32[]{:S(2)}) %all-to-all-start.6) | async-done | bytes 524320 | tf_op jit(solution)/shard_map/all_to_all | solution.py:102
  152.1 4.3 all-to-all-start.7
  158.1 8.1 %all-to-all-done.7 = bf16[4,8,16,512]{3,2,0,1:T(8,128)(2,1)} async-done(((bf16[4,8,16,512]{3,2,0,1:T(8,128)(2,1)}), bf16[4,8,16,512]{3,2,0,1:T(8,128)(2,1)}, u32[]{:S(2)}, u32[]{:S(2)}) %all-to-all-start.7) | async-done | bytes 524320 | tf_op jit(solution)/shard_map/all_to_all | solution.py:101
  167.5 4.0 scatter_fusion
  179.5 4.1 all-to-all-start.8
  189.1 7.2 %all-to-all-done.8 = bf16[4,8,16,512]{3,2,1,0:T(8,128)(2,1)} async-done(((bf16[4,8,16,512]{3,2,1,0:T(8,128)(2,1)}), bf16[4,8,16,512]{3,2,1,0:T(8,128)(2,1)}, u32[]{:S(2)}, u32[]{:S(2)}) %all-to-all-start.8) | async-done | bytes 524320 | tf_op jit(solution)/shard_map/all_to_all | solution.py:102
  198.1 4.3 all-to-all-start.9
  205.2 7.0 %all-to-all-done.9 = bf16[4,8,16,512]{3,2,0,1:T(8,128)(2,1)S(1)} async-done(((bf16[4,8,16,512]{3,2,0,1:T(8,128)(2,1)}), bf16[4,8,16,512]{3,2,0,1:T(8,128)(2,1)S(1)}, u32[]{:S(2)}, u32[]{:S(2)}) %all-to-all-start.9) | async-done | bytes 524320 | tf_op jit(solution)/shard_map/all_to_all | solution.py:101
  212.5 3.8 scatter_fusion.1
  219.5 101.3 %all-reduce.5.cloned.1.call-done = (f32[512,512]{0,1:T(8,128)}, f32[512,512]{0,1:T(8,128)}, f32[512,512]{0,1:T(8,128)}, f32[512,512]{0,1:T(8,128)}, f32[512,512]{0,1:T(8,128)}, /*index=5*/f32[512,512]{0,1:T(8,128)}) async-done(((f32[512,512]{0,1:T(8,128)}, f32[512,512]{0,1:T(8,128)}, f32[512,512]{0,1:T(8,128)}, f32[512,512]{0,1:T(8,128)}, f32[512,512]{0,1:T(8,128)}, /*index=5*/f32[512,512]{0,1:T(8,128)}), ...) | async-done | bytes 6291472 | tf_op jit(solution)/shard_map/psum | solution.py:90
  327.8 34.8 %all_to_all.63 = bf16[4,8,16,512]{3,2,1,0:T(8,128)(2,1)S(1)} all-to-all(bf16[4,8,16,512]{3,2,1,0:T(8,128)(2,1)S(1)} %copy.136), channel_id=1, replica_groups=mesh['gx'=4,'gy'=8] {'gx'}, dimensions={0} | all-to-all | bytes 1048576 | tf_op jit(solution)/shard_map/all_to_all | solution.py:102
  368.8 8.0 %all-to-all-done.11 = bf16[4,8,16,512]{3,2,0,1:T(8,128)(2,1)S(1)} async-done(((bf16[4,8,16,512]{3,2,0,1:T(8,128)(2,1)}), bf16[4,8,16,512]{3,2,0,1:T(8,128)(2,1)S(1)}, u32[]{:S(2)}, u32[]{:S(2)}) %all-to-all-start.11) | async-done | bytes 524320 | tf_op jit(solution)/shard_map/all_to_all | solution.py:101
  377.1 3.8 scatter_fusion.2
  381.6 176.1 %all-reduce.7.cloned.1.call-done = (f32[512,512]{0,1:T(8,128)}, f32[512,512]{0,1:T(8,128)}, f32[512,512]{0,1:T(8,128)}, f32[512,512]{0,1:T(8,128)}, f32[512,512]{0,1:T(8,128)}, /*index=5*/f32[512,512]{0,1:T(8,128)}) async-done(((f32[512,512]{0,1:T(8,128)}, f32[512,512]{0,1:T(8,128)}, f32[512,512]{0,1:T(8,128)}, f32[512,512]{0,1:T(8,128)}, f32[512,512]{0,1:T(8,128)}, /*index=5*/f32[512,512]{0,1:T(8,128)}), ...) | async-done | bytes 6291472 | tf_op jit(solution)/shard_map/psum | solution.py:90
  (137 shorter events, 85.3 us)
Async XLA Ops:
  7.2 41.7 %copy-start = (bf16[2,4,128,128]{3,2,1,0:T(8,128)(2,1)S(1)}, bf16[2,4,128,128]{3,2,1,0:T(8,128)(2,1)}, u32[]{:S(2)}) copy-start(bf16[2,4,128,128]{3,2,1,0:T(8,128)(2,1)} %param.14) | copy-start | bytes 786436
  12.1 25.4 %copy-start.18 = (s32[2,4]{1,0:T(2,128)S(1)}, s32[2,4]{1,0:T(2,128)}, u32[]{:S(2)}) copy-start(s32[2,4]{1,0:T(2,128)} %param.15) | copy-start | bytes 100
  12.1 25.5 %copy-start.1 = (bf16[256,512]{1,0:T(8,128)(2,1)S(1)}, bf16[256,512]{1,0:T(8,128)(2,1)}, u32[]{:S(2)}) copy-start(bf16[256,512]{1,0:T(8,128)(2,1)} %param.10) | copy-start | bytes 786436
  12.1 25.5 %copy-start.2 = (bf16[3,512,512]{2,1,0:T(8,128)(2,1)S(1)}, bf16[3,512,512]{2,1,0:T(8,128)(2,1)}, u32[]{:S(2)}) copy-start(bf16[3,512,512]{2,1,0:T(8,128)(2,1)} %param.12) | copy-start | bytes 4718596
  33.8 13.4 %all-to-all-start.1 = ((bf16[4,8,16,512]{3,2,0,1:T(8,128)(2,1)}), bf16[4,8,16,512]{3,2,0,1:T(8,128)(2,1)S(1)}, u32[]{:S(2)}, u32[]{:S(2)}) async-start(bf16[4,8,16,512]{3,2,0,1:T(8,128)(2,1)} %copy.109), calls=%async_computation.1 | async-start | bytes 1048576 | tf_op jit(solution)/shard_map/all_to_all | solution.py:56
  50.5 2.3 copy-start.8
  70.7 14.0 %all-to-all-start.3 = ((bf16[4,8,16,512]{3,2,0,1:T(8,128)(2,1)}), bf16[4,8,16,512]{3,2,0,1:T(8,128)(2,1)S(1)}, u32[]{:S(2)}, u32[]{:S(2)}) async-start(bf16[4,8,16,512]{3,2,0,1:T(8,128)(2,1)} %copy.111), calls=%async_computation.3 | async-start | bytes 1048576 | tf_op jit(solution)/shard_map/all_to_all | solution.py:56
  88.0 2.3 copy-start.10
  108.2 14.0 %all-to-all-start.5 = ((bf16[4,8,16,512]{3,2,0,1:T(8,128)(2,1)}), bf16[4,8,16,512]{3,2,0,1:T(8,128)(2,1)S(1)}, u32[]{:S(2)}, u32[]{:S(2)}) async-start(bf16[4,8,16,512]{3,2,0,1:T(8,128)(2,1)} %copy.113), calls=%async_computation.5 | async-start | bytes 1048576 | tf_op jit(solution)/shard_map/all_to_all | solution.py:56
  123.3 2.3 copy-start.12
  125.6 31.2 %copy-start.3 = (bf16[256,512]{1,0:T(8,128)(2,1)}, bf16[256,512]{1,0:T(8,128)(2,1)S(1)}, u32[]{:S(2)}) copy-start(bf16[256,512]{1,0:T(8,128)(2,1)S(1)} %multiply_convert_fusion.8) | copy-start | bytes 786436
  133.5 16.7 %all-to-all-start.6 = ((bf16[4,8,16,512]{3,2,1,0:T(8,128)(2,1)}), bf16[4,8,16,512]{3,2,1,0:T(8,128)(2,1)}, u32[]{:S(2)}, u32[]{:S(2)}) async-start(bf16[4,8,16,512]{3,2,1,0:T(8,128)(2,1)} %copy.119), calls=%async_computation.6 | async-start | bytes 1048576 | tf_op jit(solution)/shard_map/all_to_all | solution.py:102
  152.1 14.1 %all-to-all-start.7 = ((bf16[4,8,16,512]{3,2,0,1:T(8,128)(2,1)}), bf16[4,8,16,512]{3,2,0,1:T(8,128)(2,1)}, u32[]{:S(2)}, u32[]{:S(2)}) async-start(bf16[4,8,16,512]{3,2,0,1:T(8,128)(2,1)} %copy.120), calls=%async_computation.7 | async-start | bytes 1048576 | tf_op jit(solution)/shard_map/all_to_all | solution.py:101
  167.5 4.0 copy-start.14
  179.5 16.7 %all-to-all-start.8 = ((bf16[4,8,16,512]{3,2,1,0:T(8,128)(2,1)}), bf16[4,8,16,512]{3,2,1,0:T(8,128)(2,1)}, u32[]{:S(2)}, u32[]{:S(2)}) async-start(bf16[4,8,16,512]{3,2,1,0:T(8,128)(2,1)} %copy.125), calls=%async_computation.8 | async-start | bytes 1048576 | tf_op jit(solution)/shard_map/all_to_all | solution.py:102
  183.7 2.4 copy-start.4
  198.1 14.0 %all-to-all-start.9 = ((bf16[4,8,16,512]{3,2,0,1:T(8,128)(2,1)}), bf16[4,8,16,512]{3,2,0,1:T(8,128)(2,1)S(1)}, u32[]{:S(2)}, u32[]{:S(2)}) async-start(bf16[4,8,16,512]{3,2,0,1:T(8,128)(2,1)} %copy.126), calls=%async_computation.9 | async-start | bytes 1048576 | tf_op jit(solution)/shard_map/all_to_all | solution.py:101
  202.5 118.3 %all-reduce.5.cloned.1.call-start = ((), (), s32[]{:S(2)}) async-start(), calls=%async_computation.12 | async-start | bytes 12582912 | tf_op jit(solution)/shard_map/psum | solution.py:90
  212.5 3.8 copy-start.13
  212.5 4.1 copy-start.9
  219.2 338.6 %all-reduce.7.cloned.1.call-start = ((), (), s32[]{:S(2)}) async-start(), calls=%async_computation.13 | async-start | bytes 12582912 | tf_op jit(solution)/shard_map/psum | solution.py:90
  363.4 13.4 %all-to-all-start.11 = ((bf16[4,8,16,512]{3,2,0,1:T(8,128)(2,1)}), bf16[4,8,16,512]{3,2,0,1:T(8,128)(2,1)S(1)}, u32[]{:S(2)}, u32[]{:S(2)}) async-start(bf16[4,8,16,512]{3,2,0,1:T(8,128)(2,1)} %copy.137), calls=%async_computation.11 | async-start | bytes 1048576 | tf_op jit(solution)/shard_map/all_to_all | solution.py:101
  557.8 2.0 copy-start.6
  557.8 2.2 copy-start.7
  (6 other events, 8.6 us)
Sparse Core Ops, SparseCore 0:
  219.4 101.3 all-reduce.4
  323.6 234.1 all-reduce.6
